TPU v7x, 32 devices: a whole 2x2x4 slice. The times are simulated.
32 devices in a mesh: prompts: 2 (over y), patch: 4 (over z), cfg: 2 (over core), batch: 2 (over x).
Axes of the slice: x: 2, y: 2, z: 4, core: 2. Of those that a mesh axis runs over, the one named last changes fastest.
Arguments:
- latent: float32 [4, 64, 1280], P(('prompts', 'batch'), 'patch'), parts along dimension 0, may hold values from -16 to 16
- stale_keys: bfloat16 [4, 64, 1280], P('prompts', 'patch', 'batch'), parts along dimension 0, may hold values from -18 to 18
- stale_values: bfloat16 [4, 64, 1280], P('prompts', 'patch', 'batch'), parts along dimension 0, may hold values from -12 to 12
- text_keys: bfloat16 [4, 77, 1280], P(('prompts', 'cfg'), None, 'batch'), parts along dimension 0, may hold values from -160 to 160
- text_values: bfloat16 [4, 77, 1280], P(('prompts', 'cfg'), None, 'batch'), parts along dimension 0, may hold values from -6 to 6
- w_query: bfloat16 [1280, 1280], P(None, 'batch'), may hold values from -0.15625 to 0.15625
- w_key: bfloat16 [1280, 1280], P(None, 'batch'), may hold values from -0.15625 to 0.15625
- w_value: bfloat16 [1280, 1280], P(None, 'batch'), may hold values from -0.15625 to 0.15625
- w_out: bfloat16 [1280, 1280], P('batch'), may hold values from -0.15625 to 0.15625
- norm_gain: float32 [1280], replicated, may hold values from 0.25 to 1.75
- norm_bias: float32 [1280], replicated, may hold values from -0.5 to 0.5
- timesteps: int32 [6], P('prompts'), parts along dimension 0, may hold values from 0 to 999, as said below
Outputs:
- final_latent: float32 [4, 64, 1280], P(('prompts', 'batch'), 'patch'), parts along dimension 0
- final_keys: bfloat16 [4, 64, 1280], P('prompts', 'patch', 'batch'), parts along dimension 0
- final_values: bfloat16 [4, 64, 1280], P('prompts', 'patch', 'batch'), parts along dimension 0
There are 2 independent parts, one for each index of `prompts`. A program takes and returns all parts, laid end to end along the dimension named above; an argument that names none is the same for every part. Nothing has to cross between parts.
Inputs may be any that keep to these rules, and one draw needn't show every extreme that they name: `timesteps`: strictly falling from the first entry to the last.
All inputs are finite; a program needn't handle non-finite values.
Results may differ from a plain program's by a relative error of at most 0.035.
Values may be sent and summed in bfloat16 or wider, within the bound.
No kernel may reach another device: no remote copies, remote signals or barrier semaphores. Data moves between devices by JAX's collectives and lax.ppermute only.
A program may use at most 64 MiB of HBM per device.

v0:
```python
import math
import jax
import jax.numpy as jnp
from jax import lax
from jax.sharding import PartitionSpec as P

HEAD = 64
GROUPS = 32
STEPS = 2
guide_weight = 5.0
norm_eps = 1e-06


def from_partner(shard, axis, stride):
    return lax.ppermute(shard, axis, [(i, i ^ 1 << stride) for i in range(lax.axis_size(axis))])


def alpha_bar(step_index):
    grid = jnp.arange(1000, dtype=jnp.int32)
    ramp = grid.astype(jnp.float32) / 999.0
    root = math.sqrt(0.00085) + ramp * (math.sqrt(0.012) - math.sqrt(0.00085))
    logs = jnp.cumsum(jnp.log1p(-root * root))
    picked = (grid == step_index).astype(jnp.float32)
    return jnp.exp(jnp.sum(picked * logs))


def sampler_weights(now, after):
    a_now = alpha_bar(now)
    a_next = alpha_bar(after)
    keep = jnp.sqrt(a_next / a_now)
    push = jnp.sqrt(1.0 - a_next) - keep * jnp.sqrt(1.0 - a_now)
    return (keep, push)


def split_heads(block):
    return block.reshape(block.shape[0], block.shape[1], block.shape[2] // HEAD, HEAD)


def block_scores(queries, keys):
    return jnp.einsum(
        "bqhd,bkhd->bhqk", queries, keys, preferred_element_type=jnp.float32
    ) * HEAD ** (-0.5)


def body(
    latent,
    stale_keys,
    stale_values,
    text_keys,
    text_values,
    w_query,
    w_key,
    w_value,
    w_out,
    norm_gain,
    norm_bias,
    timesteps,
):
    state = latent[0]
    tok_rows = state.shape[0]
    width = state.shape[1]
    images = stale_keys.shape[0]
    local_width = w_query.shape[1]
    w_joint = jnp.concatenate([w_query, w_key, w_value], axis=1)
    patch_index = lax.axis_index("patch")
    half_index = lax.axis_index("cfg")
    group_width = width // GROUPS
    count = float(tok_rows * lax.axis_size("patch") * group_width)
    text_k = jnp.broadcast_to(text_keys, (images,) + text_keys.shape[1:])
    text_v = jnp.broadcast_to(text_values, (images,) + text_values.shape[1:])
    prior_k, prior_v = (stale_keys, stale_values)
    for step in range(STEPS):
        grouped = state.reshape(tok_rows, GROUPS, group_width)
        sums = jnp.sum(grouped, axis=(0, 2))
        squares = jnp.sum(grouped * grouped, axis=(0, 2))
        sums, squares = lax.psum((sums, squares), "patch")
        mean = sums / count
        scale = lax.rsqrt(squares / count - mean * mean + norm_eps)
        normed = ((grouped - mean[None, :, None]) * scale[None, :, None]).reshape(
            tok_rows, width
        ) * norm_gain + norm_bias
        normed = normed.astype(jnp.bfloat16)[None]
        piece = lax.all_gather(normed, "batch", axis=0, tiled=True)
        flat = piece.reshape(piece.shape[0] * tok_rows, width)
        joint_rows = jnp.dot(flat, w_joint, preferred_element_type=jnp.float32).astype(jnp.bfloat16)
        joint = joint_rows.reshape(piece.shape[0], tok_rows, 3 * local_width)
        queries = split_heads(joint[:, :, :local_width])
        fresh_k = joint[:, :, local_width : 2 * local_width]
        fresh_v = joint[:, :, 2 * local_width :]
        near_k = split_heads(jnp.concatenate([fresh_k, text_k], axis=1))
        near_v = split_heads(jnp.concatenate([fresh_v, text_v], axis=1))
        scores = block_scores(queries, near_k)
        top = jnp.max(scores, axis=-1)
        weights = jnp.exp(scores - top[..., None])
        start_acc = jnp.einsum(
            "bhqk,bkhd->bhqd",
            weights.astype(jnp.bfloat16),
            near_v,
            preferred_element_type=jnp.float32,
        )
        top_old = top
        total_old = jnp.sum(weights, axis=-1)
        piece_k = lax.all_gather(prior_k, "patch", axis=1, tiled=True)
        piece_v = lax.all_gather(prior_v, "patch", axis=1, tiled=True)
        piece_scores = block_scores(queries, split_heads(piece_k))
        place = jnp.arange(piece_k.shape[1], dtype=jnp.int32)
        own_rows = place // tok_rows == patch_index
        piece_scores = jnp.where(own_rows[None, None, None, :], -1e30, piece_scores)
        top_new = jnp.maximum(top_old, jnp.max(piece_scores, axis=-1))
        fade = jnp.exp(top_old - top_new)
        piece_weights = jnp.exp(piece_scores - top_new[..., None])
        total_new = total_old * fade + jnp.sum(piece_weights, axis=-1)
        acc_new = start_acc * fade[..., None] + jnp.einsum(
            "bhqk,bkhd->bhqd",
            piece_weights.astype(jnp.bfloat16),
            split_heads(piece_v),
            preferred_element_type=jnp.float32,
        )
        top = top_new
        attended = jnp.transpose(acc_new / total_new[..., None], (0, 2, 1, 3)).astype(jnp.bfloat16)
        attended = attended.reshape(images, tok_rows, local_width)
        rows_all = attended.reshape(images * tok_rows, local_width)
        mixed = lax.psum_scatter(
            jnp.dot(rows_all, w_out, preferred_element_type=jnp.float32).astype(jnp.bfloat16),
            "batch",
            scatter_dimension=0,
            tiled=True,
        ).astype(jnp.float32)
        branch = state + mixed
        other = from_partner(branch, "cfg", 0)
        leading = half_index == 0
        cond = jnp.where(leading, branch, other)
        uncond = jnp.where(leading, other, branch)
        guess = uncond + guide_weight * (cond - uncond)
        keep, push = sampler_weights(timesteps[step], timesteps[step + 1])
        state = keep * state + push * guess
        prior_k, prior_v = (fresh_k, fresh_v)
    return (state[None], prior_k, prior_v)


def solution(mesh):
    return jax.shard_map(
        body,
        mesh=mesh,
        in_specs=(
            P(("prompts", "batch"), "patch", None),
            P("prompts", "patch", "batch"),
            P("prompts", "patch", "batch"),
            P(("prompts", "cfg"), None, "batch"),
            P(("prompts", "cfg"), None, "batch"),
            P(None, "batch"),
            P(None, "batch"),
            P(None, "batch"),
            P("batch", None),
            P(),
            P(),
            P("prompts"),
        ),
        out_specs=(
            P(("prompts", "batch"), "patch", None),
            P("prompts", "patch", "batch"),
            P("prompts", "patch", "batch"),
        ),
        check_vma=False,
    )
```

profile of v0, /device:TPU:0, one launch (start us, length us, event | category | flops | bytes accessed | tf_op | source)
XLA Modules:
  0.0 153.0 jit_solution(90200097315867511)
XLA Ops:
  7.2 1.1 fusion.36
  8.7 13.5 %all-reduce.2 = (f32[32]{0:T(128)S(1)}, f32[32]{0:T(128)S(1)}) all-reduce(f32[32]{0:T(128)S(1)} %reduce_sum.147, f32[32]{0:T(128)S(1)} %reduce_sum.144), channel_id=1, replica_groups=mesh['prompts'=2,'patch'=4,'cfg'=2,'batch'=2] {'patch'}, use_global_device_ids=true, to_apply=%region_10.11 | all-reduce | flops 64 | bytes 512 | tf_op jit(solution)/shard_map/psum | solution.py:76
  22.6 1.1 add_convert_fusion.1
  23.6 4.7 %all_gather.18 = bf16[2,16,1280]{2,1,0:T(8,128)(2,1)S(1)} all-gather(bf16[1,16,1280]{2,1,0:T(8,128)(2,1)S(1)} %add_convert_fusion.1), channel_id=1, replica_groups=mesh['prompts'=2,'patch'=4,'cfg'=2,'batch'=2] {'batch'}, dimensions={0}, use_global_device_ids=true | all-gather | bytes 122880 | tf_op jit(solution)/shard_map/all_gather | solution.py:83
  28.3 1.6 %constant_dynamic-update-slice_fusion.2 = bf16[1280,1920]{1,0:T(8,128)(2,1)S(1)} fusion(bf16[1280,640]{1,0:T(8,128)(2,1)} %param.17), kind=kLoop, calls=%fused_computation.65 | loop fusion | bytes 3276800
  29.9 0.3 constant_dynamic-update-slice_fusion.1
  30.2 0.3 constant_dynamic-update-slice_fusion
  30.5 2.2 %copy-done.1 = bf16[1280,1920]{1,0:T(8,128)(2,1)} copy-done((bf16[1280,1920]{1,0:T(8,128)(2,1)}, bf16[1280,1920]{1,0:T(8,128)(2,1)S(1)}, u32[]{:S(2)}) %copy-start.1) | copy-done | bytes 4915224
  32.7 0.9 convolution_convert_fusion.3
  33.6 0.2 copy.65
  34.3 13.5 %all_gather.19 = bf16[2,64,640]{2,0,1:T(2,128)(2,1)S(1)} all-gather(bf16[2,16,640]{2,0,1:T(2,128)(2,1)S(1)} %copy.70), channel_id=1, replica_groups=mesh['prompts'=2,'patch'=4,'cfg'=2,'batch'=2] {'patch'}, dimensions={1}, use_global_device_ids=true | all-gather | bytes 204800 | tf_op jit(solution)/shard_map/all_gather | solution.py:103
  47.7 0.3 copy.71
  48.3 0.3 fusion.43
  48.5 0.3 fusion.44
  49.1 0.2 copy.69
  49.5 0.8 copy.74
  50.3 13.5 %all_gather.20 = bf16[2,64,640]{2,0,1:T(2,128)(2,1)S(1)} all-gather(bf16[2,16,640]{2,0,1:T(2,128)(2,1)S(1)} %copy.74), channel_id=1, replica_groups=mesh['prompts'=2,'patch'=4,'cfg'=2,'batch'=2] {'patch'}, dimensions={1}, use_global_device_ids=true | all-gather | bytes 204800 | tf_op jit(solution)/shard_map/all_gather | solution.py:104
  63.8 1.0 copy.75
  65.2 0.3 fusion.7
  65.6 1.3 fusion.8
  67.1 1.0 convolution_convert_fusion.1
  68.2 0.3 reduce-window.9
  68.8 0.6 fusion.42
  69.4 2.5 %select_reduce_fusion.2 = (f32[]{:T(128)}, f32[]{:T(128)}, f32[]{:T(128)}) fusion(f32[1024]{0:T(1024)S(1)} %add_bitcast_fusion.1, s32[]{:T(128)} %bitcast, s32[]{:T(128)} %bitcast.3, s32[]{:T(128)} %bitcast.4), kind=kLoop, calls=%fused_computation.73 | loop fusion | flops 8997 | bytes 4024 | tf_op jit(solution)/shard_map/reduce_sum | solution.py:24
  71.9 4.7 %reduce-scatter.3.cloned.1.call-done = bf16[16,1280]{1,0:T(8,128)(2,1)} async-done(((bf16[32,1280]{1,0:T(8,128)(2,1)}), bf16[16,1280]{1,0:T(8,128)(2,1)}) %reduce-scatter.3.cloned.1.call-update) | async-done | bytes 40976 | tf_op jit(solution)/shard_map/reduce_scatter | solution.py:123
  76.6 0.8 bitcast_add_fusion
  77.5 13.6 %all_gather.22 = bf16[2,64,640]{2,0,1:T(2,128)(2,1)S(1)} all-gather(bf16[2,16,640]{2,0,1:T(2,128)(2,1)S(1)} %copy.91), channel_id=1, replica_groups=mesh['prompts'=2,'patch'=4,'cfg'=2,'batch'=2] {'patch'}, dimensions={1}, use_global_device_ids=true | all-gather | bytes 204800 | tf_op jit(solution)/shard_map/all_gather | solution.py:103
  92.7 0.3 copy.81
  93.0 13.7 %all_gather.23 = bf16[2,64,640]{2,0,1:T(2,128)(2,1)S(1)} all-gather(bf16[2,16,640]{2,0,1:T(2,128)(2,1)S(1)} %copy.92), channel_id=1, replica_groups=mesh['prompts'=2,'patch'=4,'cfg'=2,'batch'=2] {'patch'}, dimensions={1}, use_global_device_ids=true | all-gather | bytes 204800 | tf_op jit(solution)/shard_map/all_gather | solution.py:104
  106.7 1.0 copy.84
  107.6 0.8 fusion.35
  108.9 11.7 %all-reduce.1 = (f32[32]{0:T(128)S(1)}, f32[32]{0:T(128)S(1)}) all-reduce(f32[32]{0:T(128)S(1)} %reduce_sum.157, f32[32]{0:T(128)S(1)} %reduce_sum.154), channel_id=1, replica_groups=mesh['prompts'=2,'patch'=4,'cfg'=2,'batch'=2] {'patch'}, use_global_device_ids=true, to_apply=%region_21.22 | all-reduce | flops 64 | bytes 512 | tf_op jit(solution)/shard_map/psum | solution.py:76
  121.0 4.7 %all-gather = bf16[32,1280]{1,0:T(8,128)(2,1)S(1)} all-gather(bf16[16,1280]{1,0:T(8,128)(2,1)S(1)} %add_convert_fusion), channel_id=2, replica_groups=mesh['prompts'=2,'patch'=4,'cfg'=2,'batch'=2] {'batch'}, dimensions={0}, use_global_device_ids=true | all-gather | bytes 122880 | tf_op jit(solution)/shard_map/all_gather | solution.py:83
  125.7 3.3 %convolution_convert_fusion.2 = bf16[32,1920]{1,0:T(8,128)(2,1)S(1)} fusion(bf16[32,1280]{1,0:T(8,128)(2,1)S(1)} %all-gather, bf16[1280,1920]{1,0:T(8,128)(2,1)} %copy-done.1), kind=kOutput, calls=%fused_computation.2 | convolution fusion | flops 157347840 | bytes 5120000 | tf_op jit(solution)/shard_map/dot_general | solution.py:85
  129.0 0.6 fusion.40
  129.7 0.6 copy-done.5
  130.3 0.2 copy.78
  130.8 0.3 fusion.45
  131.1 0.3 fusion.46
  131.4 0.2 fusion.14
  131.6 1.0 copy.80
  133.1 0.3 fusion.3
  133.4 1.3 fusion.9
  134.9 1.0 convolution_convert_fusion
  135.9 7.5 %reduce-scatter.5.cloned.1.call-done = bf16[16,1280]{1,0:T(8,128)(2,1)} async-done(((bf16[32,1280]{1,0:T(8,128)(2,1)}), bf16[16,1280]{1,0:T(8,128)(2,1)}) %reduce-scatter.5.cloned.1.call-update) | async-done | bytes 40976 | tf_op jit(solution)/shard_map/reduce_scatter | solution.py:123
  143.4 0.8 convert_add_fusion
  145.0 0.5 collective-permute-done.1
  145.5 0.7 add_bitcast_fusion
  (80 shorter events, 4.6 us)
Async XLA Ops:
  7.2 59.9 %copy-start = (bf16[640,1280]{1,0:T(8,128)(2,1)S(1)}, bf16[640,1280]{1,0:T(8,128)(2,1)}, u32[]{:S(2)}) copy-start(bf16[640,1280]{1,0:T(8,128)(2,1)} %param.20) | copy-start | bytes 4915204
  7.2 22.7 %copy-start.2 = (bf16[1280,640]{1,0:T(8,128)(2,1)S(1)}, bf16[1280,640]{1,0:T(8,128)(2,1)}, u32[]{:S(2)}) copy-start(bf16[1280,640]{1,0:T(8,128)(2,1)} %param.18) | copy-start | bytes 4915204
  7.2 69.4 %reduce-scatter.3.cloned.1.call-start = ((), (), s32[]{:S(2)}) async-start(), calls=%async_computation.2 | async-start | bytes 122880 | tf_op jit(solution)/shard_map/reduce_scatter | solution.py:123
  22.5 7.6 %copy-start.3 = (bf16[1280,640]{1,0:T(8,128)(2,1)S(1)}, bf16[1280,640]{1,0:T(8,128)(2,1)}, u32[]{:S(2)}) copy-start(bf16[1280,640]{1,0:T(8,128)(2,1)} %param.19) | copy-start | bytes 4915204
  30.2 3.7 %copy-start.6 = (bf16[1,77,640]{2,1,0:T(8,128)(2,1)S(1)}, bf16[1,77,640]{2,1,0:T(8,128)(2,1)}, u32[]{:S(2)}) copy-start(bf16[1,77,640]{2,1,0:T(8,128)(2,1)} %param.15) | copy-start | bytes 295684
  30.2 4.0 %copy-start.8 = (bf16[2,16,640]{2,1,0:T(8,128)(2,1)S(1)}, bf16[2,16,640]{2,1,0:T(8,128)(2,1)}, u32[]{:S(2)}) copy-start(bf16[2,16,640]{2,1,0:T(8,128)(2,1)} %param.13) | copy-start | bytes 122884
  30.5 2.2 %copy-start.1 = (bf16[1280,1920]{1,0:T(8,128)(2,1)}, bf16[1280,1920]{1,0:T(8,128)(2,1)S(1)}, u32[]{:S(2)}) copy-start(bf16[1280,1920]{1,0:T(8,128)(2,1)S(1)} %constant_dynamic-update-slice_fusion) | copy-start | bytes 14745604
  32.7 16.6 %copy-start.7 = (bf16[1,77,640]{2,1,0:T(8,128)(2,1)S(1)}, bf16[1,77,640]{2,1,0:T(8,128)(2,1)}, u32[]{:S(2)}) copy-start(bf16[1,77,640]{2,1,0:T(8,128)(2,1)} %param.16) | copy-start | bytes 295684
  48.0 20.7 %copy-start.11 = (s32[3]{0:T(128)S(1)}, s32[3]{0:T(128)}, u32[]{:S(2)}) copy-start(s32[3]{0:T(128)} %param.23) | copy-start | bytes 40
  48.0 28.5 %copy-start.4 = (f32[1,16,1280]{2,1,0:T(8,128)S(1)}, f32[1,16,1280]{2,1,0:T(8,128)}, u32[]{:S(2)}) copy-start(f32[1,16,1280]{2,1,0:T(8,128)} %param.12) | copy-start | bytes 245764
  48.8 72.1 %copy-start.9 = (f32[1280]{0:T(1024)S(1)}, f32[1280]{0:T(1024)}, u32[]{:S(2)}) copy-start(f32[1280]{0:T(1024)} %param.22) | copy-start | bytes 15364
  48.8 72.1 %copy-start.10 = (f32[1280]{0:T(1024)S(1)}, f32[1280]{0:T(1024)}, u32[]{:S(2)}) copy-start(f32[1280]{0:T(1024)} %param.21) | copy-start | bytes 15364
  68.1 75.3 %reduce-scatter.5.cloned.1.call-start = ((), (), s32[]{:S(2)}) async-start(), calls=%async_computation.3 | async-start | bytes 122880 | tf_op jit(solution)/shard_map/reduce_scatter | solution.py:123
  77.4 30.3 %collective-permute-start = (f32[16,1280]{1,0:T(8,128)S(1)}, f32[16,1280]{1,0:T(8,128)S(1)}, u32[]{:S(2)}, u32[]{:S(2)}) collective-permute-start(f32[16,1280]{1,0:T(8,128)S(1)} %bitcast_add_fusion), channel_id=1, source_target_pairs={{0,2},{2,0},{1,3},{3,1},{4,6},{6,4},{5,7},{7,5},{8,10},{10,8},{9,1... | collective-permute-start | bytes 245768 | tf_op jit(solution)/shard_map/ppermute | solution.py:15
  129.7 0.6 copy-start.5
  144.2 1.3 collective-permute-start.1
Sparse Core Ops, SparseCore 0:
  68.2 8.3 reduce-scatter.2
  136.1 7.2 reduce-scatter.4
where the time goes:
time: 154 us; the launch traced here: 153 us
  blocking collectives  88.9 us (58%)
  between operations  16.9 us (11%)
  local copies, waits for them, and re-layouts  13.4 us (9%)
  waiting for transfers between devices  12.7 us (8%)
  matrix products  10.7 us (7%)
  other arithmetic  10.2 us (7%)
    all_gather x2, blocking collectives, body(): piece_v = lax.all_gather(prior_v, 'patch', axis=1, tiled=True)  27.2 us
    all_gather x2, blocking collectives, body(): piece_k = lax.all_gather(prior_k, 'patch', axis=1, tiled=True)  27.1 us
    psum x2, blocking collectives, body(): sums, squares = lax.psum((sums, squares), 'patch')  25.2 us
    reduce_scatter x2, waiting for transfers between devices, body(): lax.psum_scatter(jnp.dot(rows_all, w_out, preferred_element_type=jnp.floa...  12.1 us
    all_gather x2, blocking collectives, body(): piece = lax.all_gather(normed, 'batch', axis=0, tiled=True)  9.34 us
    unnamed x30, local copies, waits for them, and re-layouts  5.64 us
    dot_general x2, matrix products, body(): jnp.dot(flat, w_joint, preferred_element_type=jnp.float32)  4.26 us
  transfers between devices with their start and end apart: 4, of which 3 were waited for; matrix products, arithmetic and copies ran while one was open for 3% of the time, Pallas kernels for 0%

commit v1 on v0

--- a/solution.py
+++ b/solution.py
@@ -80,7 +80,9 @@
             tok_rows, width
         ) * norm_gain + norm_bias
         normed = normed.astype(jnp.bfloat16)[None]
-        piece = lax.all_gather(normed, "batch", axis=0, tiled=True)
+        piece = jnp.concatenate(
+            lax.all_to_all(jnp.stack([normed] * lax.axis_size("batch")), "batch", 0, 0), axis=0
+        )
         flat = piece.reshape(piece.shape[0] * tok_rows, width)
         joint_rows = jnp.dot(flat, w_joint, preferred_element_type=jnp.float32).astype(jnp.bfloat16)
         joint = joint_rows.reshape(piece.shape[0], tok_rows, 3 * local_width)

time: 154 us -> 165 us (1.071)
  blocking collectives: 88.9 us -> 79.6 us
  starting transfers between devices: 0.22 us -> 6.86 us
  local copies, waits for them, and re-layouts: 13.4 us -> 18.7 us
  waiting for transfers between devices: 12.7 us -> 17.6 us
  matrix products: 10.7 us -> 13 us
    all_gather x2 -> x0, blocking collectives: 9.34 us -> none  [body(): piece = lax.all_gather(normed, 'batch', axis=0, tiled=True)]
    all_to_all x0 -> x2, starting transfers between devices: none -> 6.64 us  [body(): lax.all_to_all(jnp.stack([normed] * lax.axis_size('batch')), 'batch', 0, 0)]
    reduce_scatter x2, waiting for transfers between devices: 12.1 us -> 17.1 us  [body(): lax.psum_scatter(jnp.dot(rows_all, w_out, preferred_element_type=jnp.floa...]
    concatenate x1, local copies, waits for them, and re-layouts: 0.28 us -> 2.85 us  [body(): w_joint = jnp.concatenate([w_query, w_key, w_value], axis=1)]
    dot_general x2, matrix products: 4.26 us -> 6.66 us  [body(): jnp.dot(flat, w_joint, preferred_element_type=jnp.float32)]
    unnamed x30 -> x28, local copies, waits for them, and re-layouts: 5.64 us -> 6.59 us
  transfers between devices with their start and end apart: 4 -> 6, of which waited for: 3 -> 3; matrix products, arithmetic and copies ran while one was open for 3% -> 12% of each run, Pallas kernels for 0% -> 0%
where the time goes in v1:
time: 165 us; the launch traced here: 164 us
  blocking collectives  79.6 us (48%)
  local copies, waits for them, and re-layouts  18.7 us (11%)
  waiting for transfers between devices  17.6 us (11%)
  between operations  16.8 us (10%)
  matrix products  13 us (8%)
  other arithmetic  11.4 us (7%)
  starting transfers between devices  6.86 us (4%)
    all_gather x2, blocking collectives, body(): piece_v = lax.all_gather(prior_v, 'patch', axis=1, tiled=True)  27.1 us
    all_gather x2, blocking collectives, body(): piece_k = lax.all_gather(prior_k, 'patch', axis=1, tiled=True)  27.1 us
    psum x2, blocking collectives, body(): sums, squares = lax.psum((sums, squares), 'patch')  25.4 us
    reduce_scatter x2, waiting for transfers between devices, body(): lax.psum_scatter(jnp.dot(rows_all, w_out, preferred_element_type=jnp.floa...  17.1 us
    dot_general x2, matrix products, body(): jnp.dot(flat, w_joint, preferred_element_type=jnp.float32)  6.66 us
    all_to_all x2, starting transfers between devices, body(): lax.all_to_all(jnp.stack([normed] * lax.axis_size('batch')), 'batch', 0, 0)  6.64 us
    unnamed x28, local copies, waits for them, and re-layouts  6.59 us
  transfers between devices with their start and end apart: 6, of which 3 were waited for; matrix products, arithmetic and copies ran while one was open for 12% of the time, Pallas kernels for 0%

profile of v1, /device:TPU:0, one launch (start us, length us, event | category | flops | bytes accessed | tf_op | source)
XLA Modules:
  0.0 164.2 jit_solution(17580894439408109156)
XLA Ops:
  7.2 1.1 fusion.41
  8.7 13.5 %all-reduce.2 = (f32[32]{0:T(128)S(1)}, f32[32]{0:T(128)S(1)}) all-reduce(f32[32]{0:T(128)S(1)} %reduce_sum.147, f32[32]{0:T(128)S(1)} %reduce_sum.144), channel_id=1, replica_groups=mesh['prompts'=2,'patch'=4,'cfg'=2,'batch'=2] {'patch'}, use_global_device_ids=true, to_apply=%region_10.11 | all-reduce | flops 64 | bytes 512 | tf_op jit(solution)/shard_map/psum | solution.py:76
  22.5 0.9 fusion.25
  23.4 0.6 pad_maximum_fusion.4
  24.1 3.3 %all-to-all-start = ((bf16[2,1,16,1280]{3,2,1,0:T(8,128)(2,1)}), bf16[2,1,16,1280]{3,2,1,0:T(8,128)(2,1)S(1)}, u32[]{:S(2)}, u32[]{:S(2)}) async-start(bf16[2,1,16,1280]{3,2,1,0:T(8,128)(2,1)} %pad_maximum_fusion.4), calls=%async_computation | async-start | bytes 163840 | tf_op jit(solution)/shard_map/all_to_all | solution.py:84
  27.5 2.9 %constant_dynamic-update-slice_fusion.2 = bf16[1280,1920]{1,0:T(8,128)(2,1)} fusion(bf16[1280,640]{1,0:T(8,128)(2,1)} %param.17), kind=kLoop, calls=%fused_computation.72 | loop fusion | bytes 3276800
  30.3 1.7 %copy.64 = bf16[77,640]{0,1:T(8,128)(2,1)} copy(bf16[77,640]{1,0:T(8,128)(2,1)} %bitcast.119) | data formatting | bytes 197120 | tf_op jit(solution)/shard_map/broadcast_in_dim | solution.py:69
  32.0 0.8 copy.70
  32.8 13.5 %all_gather.12 = bf16[2,64,640]{2,0,1:T(2,128)(2,1)S(1)} all-gather(bf16[2,16,640]{2,0,1:T(2,128)(2,1)S(1)} %copy.70), channel_id=1, replica_groups=mesh['prompts'=2,'patch'=4,'cfg'=2,'batch'=2] {'patch'}, dimensions={1}, use_global_device_ids=true | all-gather | bytes 204800 | tf_op jit(solution)/shard_map/all_gather | solution.py:105
  46.3 1.0 copy.71
  47.3 1.1 copy.68
  48.3 1.4 copy.74
  49.8 0.3 reduce-window.9
  50.3 1.4 constant_dynamic-update-slice_fusion.1
  51.7 2.9 %constant_dynamic-update-slice_fusion = bf16[1280,1920]{1,0:T(8,128)(2,1)} fusion(bf16[1280,1920]{1,0:T(8,128)(2,1)} %constant_dynamic-update-slice_fusion.1, bf16[1280,640]{1,0:T(8,128)(2,1)} %param.19), kind=kLoop, calls=%fused_computation.70 | loop fusion | bytes 3276800 | tf_op jit(solution)/shard_map/concatenate | solution.py:64
  54.5 13.6 %all_gather.13 = bf16[2,64,640]{2,0,1:T(2,128)(2,1)S(1)} all-gather(bf16[2,16,640]{2,0,1:T(2,128)(2,1)S(1)} %copy-done.5), channel_id=1, replica_groups=mesh['prompts'=2,'patch'=4,'cfg'=2,'batch'=2] {'patch'}, dimensions={1}, use_global_device_ids=true | all-gather | bytes 204800 | tf_op jit(solution)/shard_map/all_gather | solution.py:106
  68.1 0.9 copy.75
  69.1 3.3 %convolution_convert_fusion.3 = bf16[32,1920]{1,0:T(8,128)(2,1)S(1)} fusion(bf16[32,1280]{1,0:T(8,128)(2,1)S(1)} %bitcast.117, bf16[1280,1920]{1,0:T(8,128)(2,1)} %constant_dynamic-update-slice_fusion), kind=kOutput, calls=%fused_computation.3 | convolution fusion | flops 157347840 | bytes 5120000 | tf_op jit(solution)/shard_map/dot_general | solution.py:87
  72.5 0.2 copy.65
  73.1 0.3 fusion.48
  73.4 0.3 fusion.49
  74.6 0.3 fusion.7
  74.9 1.3 fusion.8
  76.5 1.0 convolution_convert_fusion.1
  77.5 0.7 fusion.47
  78.2 8.2 %reduce-scatter.3.cloned.1.call-done = bf16[16,1280]{1,0:T(8,128)(2,1)} async-done(((bf16[32,1280]{1,0:T(8,128)(2,1)}), bf16[16,1280]{1,0:T(8,128)(2,1)}) %reduce-scatter.3.cloned.1.call-update) | async-done | bytes 40976 | tf_op jit(solution)/shard_map/reduce_scatter | solution.py:125
  86.4 0.8 bitcast_add_fusion
  87.3 2.6 %select_reduce_fusion.2 = (f32[]{:T(128)}, f32[]{:T(128)}, f32[]{:T(128)}) fusion(f32[1024]{0:T(1024)S(1)} %add_bitcast_fusion.1, s32[]{:T(128)} %bitcast, s32[]{:T(128)} %bitcast.3, s32[]{:T(128)} %bitcast.4), kind=kLoop, calls=%fused_computation.80 | loop fusion | flops 8997 | bytes 4024 | tf_op jit(solution)/shard_map/reduce_sum | solution.py:24
  91.4 13.6 %all_gather.14 = bf16[2,64,640]{2,0,1:T(2,128)(2,1)S(1)} all-gather(bf16[2,16,640]{2,0,1:T(2,128)(2,1)S(1)} %copy.91), channel_id=1, replica_groups=mesh['prompts'=2,'patch'=4,'cfg'=2,'batch'=2] {'patch'}, dimensions={1}, use_global_device_ids=true | all-gather | bytes 204800 | tf_op jit(solution)/shard_map/all_gather | solution.py:105
  105.0 0.3 copy.81
  105.3 0.8 fusion.40
  106.5 12.0 %all-reduce.1 = (f32[32]{0:T(128)S(1)}, f32[32]{0:T(128)S(1)}) all-reduce(f32[32]{0:T(128)S(1)} %reduce_sum.157, f32[32]{0:T(128)S(1)} %reduce_sum.154), channel_id=1, replica_groups=mesh['prompts'=2,'patch'=4,'cfg'=2,'batch'=2] {'patch'}, use_global_device_ids=true, to_apply=%region_21.22 | all-reduce | flops 64 | bytes 512 | tf_op jit(solution)/shard_map/psum | solution.py:76
  118.9 0.6 pad_maximum_fusion.5
  119.5 3.3 %all-to-all-start.1 = ((bf16[2,1,16,1280]{3,2,1,0:T(8,128)(2,1)}), bf16[2,1,16,1280]{3,2,1,0:T(8,128)(2,1)S(1)}, u32[]{:S(2)}, u32[]{:S(2)}) async-start(bf16[2,1,16,1280]{3,2,1,0:T(8,128)(2,1)} %pad_maximum_fusion.5), calls=%async_computation.2 | async-start | bytes 163840 | tf_op jit(solution)/shard_map/all_to_all | solution.py:84
  122.9 13.5 %all_gather.15 = bf16[2,64,640]{2,0,1:T(2,128)(2,1)S(1)} all-gather(bf16[2,16,640]{2,0,1:T(2,128)(2,1)S(1)} %copy.92), channel_id=1, replica_groups=mesh['prompts'=2,'patch'=4,'cfg'=2,'batch'=2] {'patch'}, dimensions={1}, use_global_device_ids=true | all-gather | bytes 204800 | tf_op jit(solution)/shard_map/all_gather | solution.py:106
  136.4 1.0 copy.84
  137.4 3.3 %convolution_convert_fusion.2 = bf16[32,1920]{1,0:T(8,128)(2,1)S(1)} fusion(bf16[32,1280]{1,0:T(8,128)(2,1)S(1)} %bitcast.118, bf16[1280,1920]{1,0:T(8,128)(2,1)} %constant_dynamic-update-slice_fusion), kind=kOutput, calls=%fused_computation.2 | convolution fusion | flops 157347840 | bytes 5120000 | tf_op jit(solution)/shard_map/dot_general | solution.py:87
  140.7 0.2 copy.78
  141.3 0.3 fusion.50
  141.6 0.3 fusion.51
  142.1 0.2 copy.80
  142.8 0.3 fusion.3
  143.1 1.3 fusion.9
  144.6 1.0 convolution_convert_fusion
  145.6 8.9 %reduce-scatter.5.cloned.1.call-done = bf16[16,1280]{1,0:T(8,128)(2,1)} async-done(((bf16[32,1280]{1,0:T(8,128)(2,1)}), bf16[16,1280]{1,0:T(8,128)(2,1)}) %reduce-scatter.5.cloned.1.call-update) | async-done | bytes 40976 | tf_op jit(solution)/shard_map/reduce_scatter | solution.py:125
  154.5 0.8 convert_add_fusion
  156.2 0.5 collective-permute-done.1
  156.6 0.7 add_bitcast_fusion
  (82 shorter events, 4.7 us)
Async XLA Ops:
  7.2 69.3 %copy-start = (bf16[640,1280]{1,0:T(8,128)(2,1)S(1)}, bf16[640,1280]{1,0:T(8,128)(2,1)}, u32[]{:S(2)}) copy-start(bf16[640,1280]{1,0:T(8,128)(2,1)} %param.20) | copy-start | bytes 4915204
  7.2 43.1 %copy-start.1 = (bf16[1280,640]{1,0:T(8,128)(2,1)S(1)}, bf16[1280,640]{1,0:T(8,128)(2,1)}, u32[]{:S(2)}) copy-start(bf16[1280,640]{1,0:T(8,128)(2,1)} %param.18) | copy-start | bytes 4915204
  24.1 45.0 %all-to-all-start = ((bf16[2,1,16,1280]{3,2,1,0:T(8,128)(2,1)}), bf16[2,1,16,1280]{3,2,1,0:T(8,128)(2,1)S(1)}, u32[]{:S(2)}, u32[]{:S(2)}) async-start(bf16[2,1,16,1280]{3,2,1,0:T(8,128)(2,1)} %pad_maximum_fusion.4), calls=%async_computation | async-start | bytes 163840 | tf_op jit(solution)/shard_map/all_to_all | solution.py:84
  27.4 59.0 %reduce-scatter.3.cloned.1.call-start = ((), (), s32[]{:S(2)}) async-start(), calls=%async_computation.4 | async-start | bytes 122880 | tf_op jit(solution)/shard_map/reduce_scatter | solution.py:125
  50.2 4.3 %copy-start.5 = (bf16[2,16,640]{2,0,1:T(2,128)(2,1)S(1)}, bf16[2,16,640]{2,0,1:T(2,128)(2,1)}, u32[]{:S(2)}) copy-start(bf16[2,16,640]{2,0,1:T(2,128)(2,1)} %copy.74) | copy-start | bytes 122884
  51.6 21.2 %copy-start.4 = (bf16[77,640]{0,1:T(8,128)(2,1)S(1)}, bf16[77,640]{0,1:T(8,128)(2,1)}, u32[]{:S(2)}) copy-start(bf16[77,640]{0,1:T(8,128)(2,1)} %copy.64) | copy-start | bytes 295684
  54.5 18.9 %copy-start.3 = (bf16[2,64,640]{1,2,0:T(8,128)(2,1)S(1)}, bf16[2,64,640]{1,2,0:T(8,128)(2,1)}, u32[]{:S(2)}) copy-start(bf16[2,64,640]{1,2,0:T(8,128)(2,1)} %copy.71) | copy-start | bytes 491524
  72.4 5.1 %copy-start.10 = (s32[3]{0:T(128)S(1)}, s32[3]{0:T(128)}, u32[]{:S(2)}) copy-start(s32[3]{0:T(128)} %param.23) | copy-start | bytes 40
  72.4 14.0 %copy-start.2 = (f32[1,16,1280]{2,1,0:T(8,128)S(1)}, f32[1,16,1280]{2,1,0:T(8,128)}, u32[]{:S(2)}) copy-start(f32[1,16,1280]{2,1,0:T(8,128)} %param.12) | copy-start | bytes 245764
  72.9 46.0 %copy-start.8 = (f32[1280]{0:T(1024)S(1)}, f32[1280]{0:T(1024)}, u32[]{:S(2)}) copy-start(f32[1280]{0:T(1024)} %param.22) | copy-start | bytes 15364
  72.9 46.0 %copy-start.9 = (f32[1280]{0:T(1024)S(1)}, f32[1280]{0:T(1024)}, u32[]{:S(2)}) copy-start(f32[1280]{0:T(1024)} %param.21) | copy-start | bytes 15364
  87.2 18.1 %collective-permute-start = (f32[16,1280]{1,0:T(8,128)S(1)}, f32[16,1280]{1,0:T(8,128)S(1)}, u32[]{:S(2)}, u32[]{:S(2)}) collective-permute-start(f32[16,1280]{1,0:T(8,128)S(1)} %bitcast_add_fusion), channel_id=1, source_target_pairs={{0,2},{2,0},{1,3},{3,1},{4,6},{6,4},{5,7},{7,5},{8,10},{10,8},{9,1... | collective-permute-start | bytes 245768 | tf_op jit(solution)/shard_map/ppermute | solution.py:15
  119.5 17.8 %all-to-all-start.1 = ((bf16[2,1,16,1280]{3,2,1,0:T(8,128)(2,1)}), bf16[2,1,16,1280]{3,2,1,0:T(8,128)(2,1)S(1)}, u32[]{:S(2)}, u32[]{:S(2)}) async-start(bf16[2,1,16,1280]{3,2,1,0:T(8,128)(2,1)} %pad_maximum_fusion.5), calls=%async_computation.2 | async-start | bytes 163840 | tf_op jit(solution)/shard_map/all_to_all | solution.py:84
  122.9 31.7 %reduce-scatter.5.cloned.1.call-start = ((), (), s32[]{:S(2)}) async-start(), calls=%async_computation.5 | async-start | bytes 122880 | tf_op jit(solution)/shard_map/reduce_scatter | solution.py:125
  140.7 16.6 %copy-start.6 = (bf16[2,16,640]{2,1,0:T(8,128)(2,1)}, bf16[2,16,640]{2,1,0:T(8,128)(2,1)S(1)}, u32[]{:S(2)}) copy-start(bf16[2,16,640]{2,1,0:T(8,128)(2,1)S(1)} %get-tuple-element.20) | copy-start | bytes 122884
  140.7 16.6 %copy-start.7 = (bf16[2,16,640]{2,1,0:T(8,128)(2,1)}, bf16[2,16,640]{2,1,0:T(8,128)(2,1)S(1)}, u32[]{:S(2)}) copy-start(bf16[2,16,640]{2,1,0:T(8,128)(2,1)S(1)} %get-tuple-element.21) | copy-start | bytes 122884
  155.3 1.3 collective-permute-start.1
Sparse Core Ops, SparseCore 0:
  77.6 8.7 reduce-scatter.2
  145.8 8.7 reduce-scatter.4
